TPU v7x, 256 devices: a whole 4x4x8 slice. The times are simulated.
256 devices in a mesh: tm: 8 (over y, core), head: 32 (over z, x).
Axes of the slice: x: 4, y: 4, z: 8, core: 2. Of those that a mesh axis runs over, the one named last changes fastest.
Arguments:
- tokens: bfloat16 [4096, 5120], P('tm'), may hold values from -24 to 24
- w_query: bfloat16 [5120, 4096], P(None, 'head'), may hold values from -0.078125 to 0.078125
- w_key: bfloat16 [5120, 4096], P(None, 'head'), may hold values from -0.078125 to 0.078125
- w_value: bfloat16 [5120, 4096], P(None, 'head'), may hold values from -0.078125 to 0.078125
- w_out: bfloat16 [4096, 5120], P('head'), may hold values from -0.09375 to 0.09375
- out_grad: bfloat16 [4096, 5120], P('tm'), may hold values from -6 to 6
- frame_lists: int32 [8, 8], replicated, may hold values from 0 to 1, as said below
Outputs:
- token_grad: bfloat16 [4096, 5120], P(('tm', 'head'))
- query_grad: bfloat16 [5120, 4096], P('tm', 'head')
- key_grad: bfloat16 [5120, 4096], P('tm', 'head')
- value_grad: bfloat16 [5120, 4096], P('tm', 'head')
- out_weight_grad: bfloat16 [4096, 5120], P('head', 'tm')
Inputs may be any that keep to these rules, and one draw needn't show every extreme that they name: `frame_lists`: entries with j >= i are 0; entry (i, i - 1) is 1 for every group i > 0.
All inputs are finite; a program needn't handle non-finite values.
Results may differ from a plain program's by a relative error of at most 0.02.
The roundings to bfloat16 on the way count: a program that leaves them out, or rounds other values in their place, can miss the bound.
Values may be sent and summed in bfloat16 or wider, within the bound.
A program may use at most 128 MiB of HBM per device.

v0:
```python
import jax
import jax.numpy as jnp
from jax import lax
from jax.sharding import PartitionSpec as P


def contract_rows(left, right):
    return lax.dot_general(
        left, right, (((0,), (0,)), ((), ())), preferred_element_type=jnp.float32
    )


def contract_cols(left, right):
    return lax.dot_general(
        left, right, (((1,), (1,)), ((), ())), preferred_element_type=jnp.float32
    )


def local(tokens, w_query, w_key, w_value, w_out, out_grad, frame_lists):
    width = w_query.shape[1]
    scale = 1.0 / width**0.5
    rows = tokens.shape[0]
    groups = lax.axis_size("tm")
    mine = lax.axis_index("tm")
    query = jnp.dot(tokens, w_query, preferred_element_type=jnp.float32).astype(jnp.bfloat16)
    keys = jnp.dot(tokens, w_key, preferred_element_type=jnp.float32).astype(jnp.bfloat16)
    values = jnp.dot(tokens, w_value, preferred_element_type=jnp.float32).astype(jnp.bfloat16)
    d_attn = contract_cols(out_grad, w_out).astype(jnp.bfloat16)
    my_list = lax.dynamic_slice_in_dim(frame_lists, mine, 1, 0)[0]
    key_all, value_all = (
        lax.all_gather(keys, "tm", axis=0, tiled=True),
        lax.all_gather(values, "tm", axis=0, tiled=True),
    )
    order = jnp.arange(groups, dtype=jnp.int32)
    allowed = (order == mine) | (my_list == 1) & (order < mine)
    key_mask = jnp.repeat(allowed, rows)[None, :]
    scores = contract_cols(query, key_all) * scale
    scores = jnp.where(key_mask, scores, jnp.float32(-1e30))
    top = jnp.max(scores, axis=1, keepdims=True)
    expd = jnp.exp(scores - top)
    probs = expd / jnp.sum(expd, axis=1, keepdims=True)
    probs_b = probs.astype(jnp.bfloat16)
    attn = jnp.dot(probs_b, value_all, preferred_element_type=jnp.float32).astype(jnp.bfloat16)
    dprobs = contract_cols(d_attn, value_all)
    delta = jnp.sum(probs * dprobs, axis=1, keepdims=True)
    dscore = (probs * (dprobs - delta) * scale).astype(jnp.bfloat16)
    dquery = jnp.dot(dscore, key_all, preferred_element_type=jnp.float32).astype(jnp.bfloat16)
    cache_terms = jnp.concatenate(
        [contract_rows(dscore, query), contract_rows(probs_b, d_attn)], axis=1
    )
    summed = lax.psum_scatter(
        cache_terms.astype(jnp.bfloat16), "tm", scatter_dimension=0, tiled=True
    ).astype(jnp.float32)
    dkey = summed[:, :width].astype(jnp.bfloat16)
    dvalue = summed[:, width:].astype(jnp.bfloat16)
    weights_sum = lax.psum_scatter(
        jnp.concatenate(
            [
                contract_rows(tokens, dquery),
                contract_rows(tokens, dkey),
                contract_rows(tokens, dvalue),
                contract_rows(out_grad, attn),
            ],
            axis=1,
        ).astype(jnp.bfloat16),
        "tm",
        scatter_dimension=0,
        tiled=True,
    ).astype(jnp.float32)
    query_grad = weights_sum[:, :width].astype(jnp.bfloat16)
    key_grad = weights_sum[:, width : 2 * width].astype(jnp.bfloat16)
    value_grad = weights_sum[:, 2 * width : 3 * width].astype(jnp.bfloat16)
    out_weight_grad = weights_sum[:, 3 * width :].T.astype(jnp.bfloat16)
    token_grad = lax.psum_scatter(
        (
            contract_cols(dquery, w_query)
            + contract_cols(dkey, w_key)
            + contract_cols(dvalue, w_value)
        ).astype(jnp.bfloat16),
        "head",
        scatter_dimension=0,
        tiled=True,
    )
    return (token_grad, query_grad, key_grad, value_grad, out_weight_grad)


def solution(mesh):
    in_specs = (
        P("tm", None),
        P(None, "head"),
        P(None, "head"),
        P(None, "head"),
        P("head", None),
        P("tm", None),
        P(),
    )
    out_specs = (
        P(("tm", "head"), None),
        P("tm", "head"),
        P("tm", "head"),
        P("tm", "head"),
        P("head", "tm"),
    )
    return jax.shard_map(local, mesh=mesh, in_specs=in_specs, out_specs=out_specs, check_vma=False)
```

profile of v0, /device:TPU:8, one launch (start us, length us, event | category | flops | bytes accessed | tf_op | source)
XLA Modules:
  0.0 424.9 jit_solution(9849481897770291235)
XLA Ops:
  7.2 0.0 copy-start
  7.2 0.0 copy-start.7
  7.2 0.0 all-gather.3.cloned.1.call-start
  7.2 5.2 %convolution_convert_fusion.9 = bf16[512,128]{1,0:T(8,128)(2,1)} fusion(bf16[512,5120]{1,0:T(8,128)(2,1)} %param.7, bf16[5120,128]{1,0:T(8,128)(2,1)} %param.9), kind=kOutput, calls=%fused_computation.26 | convolution fusion | flops 671154176 | bytes 6684672 | tf_op jit(solution)/shard_map/dot_general | solution.py:26
  12.4 0.0 all-gather.3.cloned.1.call-update
  12.5 0.0 all-gather.5.cloned.1.call-start
  12.5 0.0 copy-done.7
  12.5 4.7 %convolution_convert_fusion.7 = bf16[512,128]{1,0:T(8,128)(2,1)} fusion(bf16[512,5120]{1,0:T(8,128)(2,1)} %param.7, bf16[5120,128]{1,0:T(8,128)(2,1)S(1)} %copy-done.7), kind=kOutput, calls=%fused_computation.24 | convolution fusion | flops 671154176 | bytes 6684672 | tf_op jit(solution)/shard_map/dot_general | solution.py:27
  17.2 0.0 copy-start.9
  17.2 0.0 all-gather.5.cloned.1.call-update
  17.2 0.0 reduce-scatter.6.cloned.1.call-start
  17.3 0.8 fusion.20
  18.0 0.1 broadcast_bitcast_fusion
  18.1 0.0 copy-done
  18.1 4.0 convolution_convert_fusion.10
  22.1 0.0 copy-done.9
  22.2 4.0 convolution_convert_fusion.8
  26.2 13.5 %all-gather.3.cloned.1.call-done = bf16[4096,128]{1,0:T(8,128)(2,1)} async-done(((bf16[512,128]{1,0:T(8,128)(2,1)}), bf16[4096,128]{1,0:T(8,128)(2,1)}) %all-gather.3.cloned.1.call-update) | async-done | bytes 1048592 | tf_op jit(solution)/shard_map/all_gather | solution.py:31
  39.7 2.7 fusion
  42.5 0.0 copy-start.2
  42.5 3.2 copy-done.2
  45.7 2.2 fusion.2
  47.9 20.2 %all-gather.5.cloned.1.call-done = bf16[4096,128]{1,0:T(8,128)(2,1)} async-done(((bf16[512,128]{1,0:T(8,128)(2,1)}), bf16[4096,128]{1,0:T(8,128)(2,1)}) %all-gather.5.cloned.1.call-update) | async-done | bytes 1048592 | tf_op jit(solution)/shard_map/all_gather | solution.py:32
  68.0 7.4 %multiply_reduce_fusion = (f32[512]{0:T(512)S(1)}, f32[512,4096]{1,0:T(8,128)S(1)}, f32[512,4096]{1,0:T(8,128)}) fusion(f32[512]{0:T(512)S(1)} %fusion.2, f32[512]{0:T(512)S(1)} %get-tuple-element.21, f32[512,4096]{1,0:T(8,128)} %copy-done.2, pred[4096]{0:T(1024)(128)(4,1)S(1)} %bitcast.47, bf16[512,128]{1,0:T(8,128)(2,1)S(1)} %convolution_convert_fusion.8, ...), kind=kOutput, calls=%fused_computation.2 | convolution fusion | flops 549453312 | bytes 26355712 | tf_op jit(solution)/shard_map/dot_general | solution.py:14
  75.4 0.0 copy-start.1
  75.5 0.8 convolution_convert_fusion.4
  76.2 2.5 copy-done.1
  78.7 8.0 %multiply_convert_fusion = bf16[512,4096]{1,0:T(8,128)(2,1)S(1)} fusion(f32[512,4096]{1,0:T(8,128)} %copy-done.1, f32[512,4096]{1,0:T(8,128)} %get-tuple-element.23, f32[512]{0:T(512)S(1)} %get-tuple-element.15), kind=kLoop, calls=%fused_computation.1 | loop fusion | flops 8388608 | bytes 20973568 | tf_op jit(solution)/shard_map/convert_element_type | solution.py:46
  86.7 0.0 copy-start.3
  86.7 2.0 copy-done.3
  88.7 0.8 convolution_convert_fusion.5
  89.5 1.5 pad_maximum_fusion.1
  90.9 0.0 reduce-scatter.6.cloned.1.call-update
  91.0 0.2 reduce-scatter.10.cloned.1.call-start
  91.2 3.7 convolution_convert_fusion.6
  94.9 3.4 fusion.3
  98.3 9.7 %fusion.6 = bf16[5120,128]{0,1:T(8,128)(2,1)} fusion(bf16[512,5120]{1,0:T(8,128)(2,1)} %param.12, bf16[4096,128]{1,0:T(8,128)(2,1)} %all-gather.5.cloned.1.call-done, f32[512,4096]{1,0:T(8,128)} %copy-done.1), kind=kOutput, calls=%fused_computation.15 | convolution fusion | flops 1210777600 | bytes 15990784 | tf_op jit(solution)/shard_map/dot_general | solution.py:8
  108.0 17.6 %reduce-scatter.6.cloned.1.call-done = bf16[512,256]{0,1:T(8,128)(2,1)} async-done(((bf16[4096,256]{0,1:T(8,128)(2,1)}), bf16[512,256]{0,1:T(8,128)(2,1)}) %reduce-scatter.6.cloned.1.call-update) | async-done | bytes 262160 | tf_op jit(solution)/shard_map/reduce_scatter | solution.py:51
  125.6 0.0 copy-start.5
  125.6 3.5 fusion.4
  129.1 0.0 copy-done.5
  129.1 0.0 copy-start.4
  129.1 3.4 fusion.5
  132.5 0.0 copy-done.4
  132.6 3.5 pad_maximum_fusion
  136.1 7.9 %copy.18 = bf16[5120,512]{1,0:T(8,128)(2,1)} copy(bf16[5120,512]{0,1:T(8,128)(2,1)} %pad_maximum_fusion) | data formatting | bytes 10485760
  144.0 0.0 reduce-scatter.10.cloned.1.call-update
  144.0 0.0 copy-start.6
  144.0 0.0 reduce-scatter.8.cloned.1.call-start
  144.1 1.5 fusion.23
  145.6 0.0 copy-done.6
  145.6 0.0 copy-start.8
  145.6 5.5 %fusion.18 = f32[512,5120]{1,0:T(8,128)} fusion(bf16[5120,128]{1,0:T(8,128)(2,1)S(1)} %copy-done.6, bf16[512,256]{0,1:T(8,128)(2,1)S(1)} %copy-done.5), kind=kOutput, calls=%fused_computation.32 | convolution fusion | flops 671088640 | bytes 11927552 | tf_op jit(solution)/shard_map/dot_general | solution.py:14
  151.2 0.0 copy-done.8
  151.2 8.2 %add_convert_fusion = bf16[512,5120]{1,0:T(8,128)(2,1)} fusion(f32[512,5120]{1,0:T(8,128)S(1)} %fusion.23, f32[512,5120]{1,0:T(8,128)} %fusion.18, bf16[5120,128]{1,0:T(8,128)(2,1)S(1)} %copy-done.8, bf16[512,256]{0,1:T(8,128)(2,1)S(1)} %copy-done.5), kind=kOutput, calls=%fused_computation | convolution fusion | flops 678952960 | bytes 27656192 | tf_op jit(solution)/shard_map/dot_general | solution.py:14
  159.3 0.0 reduce-scatter.8.cloned.1.call-update
  159.4 25.7 %reduce-scatter.10.cloned.1.call-done = bf16[640,512]{1,0:T(8,128)(2,1)} async-done(((bf16[5120,512]{1,0:T(8,128)(2,1)}), bf16[640,512]{1,0:T(8,128)(2,1)}) %reduce-scatter.10.cloned.1.call-update) | async-done | bytes 655376
  185.1 2.0 fusion.22
  187.0 0.8 copy.23
  187.8 230.5 %reduce-scatter.8.cloned.1.call-done = bf16[16,5120]{1,0:T(8,128)(2,1)} async-done(((bf16[512,5120]{1,0:T(8,128)(2,1)}), bf16[16,5120]{1,0:T(8,128)(2,1)}) %reduce-scatter.8.cloned.1.call-update) | async-done | bytes 163856 | tf_op jit(solution)/shard_map/reduce_scatter | solution.py:74
  (1 shorter events, 0.0 us)
Async XLA Ops:
  7.2 11.0 %copy-start = (bf16[5120,128]{1,0:T(8,128)(2,1)S(1)}, bf16[5120,128]{1,0:T(8,128)(2,1)}, u32[]{:S(2)}) copy-start(bf16[5120,128]{1,0:T(8,128)(2,1)} %param.8) | copy-start | bytes 3932164
  7.2 5.3 %copy-start.7 = (bf16[5120,128]{1,0:T(8,128)(2,1)S(1)}, bf16[5120,128]{1,0:T(8,128)(2,1)}, u32[]{:S(2)}) copy-start(bf16[5120,128]{1,0:T(8,128)(2,1)} %param.10) | copy-start | bytes 3932164
  7.2 32.6 %all-gather.3.cloned.1.call-start = ((), (), s32[]{:S(2)}) async-start(), calls=%async_computation.3 | async-start | bytes 1179648 | tf_op jit(solution)/shard_map/all_gather | solution.py:31
  12.5 55.6 %all-gather.5.cloned.1.call-start = ((), (), s32[]{:S(2)}) async-start(), calls=%async_computation.4 | async-start | bytes 1179648 | tf_op jit(solution)/shard_map/all_gather | solution.py:32
  17.2 5.0 %copy-start.9 = (bf16[128,5120]{1,0:T(8,128)(2,1)S(1)}, bf16[128,5120]{1,0:T(8,128)(2,1)}, u32[]{:S(2)}) copy-start(bf16[128,5120]{1,0:T(8,128)(2,1)} %param.11) | copy-start | bytes 3932164
  17.2 108.4 %reduce-scatter.6.cloned.1.call-start = ((), (), s32[]{:S(2)}) async-start(), calls=%async_computation.5 | async-start | bytes 2359296 | tf_op jit(solution)/shard_map/reduce_scatter | solution.py:51
  42.5 3.2 copy-start.2
  75.4 3.2 copy-start.1
  86.7 2.0 copy-start.3
  91.0 94.1 %reduce-scatter.10.cloned.1.call-start = ((), (), s32[]{:S(2)}) async-start(), calls=%async_computation.7 | async-start | bytes 5898240
  125.6 3.5 copy-start.5
  129.1 3.5 copy-start.4
  144.0 1.6 copy-start.6
  144.0 274.3 %reduce-scatter.8.cloned.1.call-start = ((), (), s32[]{:S(2)}) async-start(), calls=%async_computation.6 | async-start | bytes 5406720 | tf_op jit(solution)/shard_map/reduce_scatter | solution.py:74
  145.6 5.5 %copy-start.8 = (bf16[5120,128]{1,0:T(8,128)(2,1)S(1)}, bf16[5120,128]{1,0:T(8,128)(2,1)}, u32[]{:S(2)}) copy-start(bf16[5120,128]{1,0:T(8,128)(2,1)} %param.10) | copy-start | bytes 3932164
Sparse Core Ops, SparseCore 0:
  12.6 27.1 all-gather.2
  42.2 25.7 all-gather.4
  91.1 34.4 reduce-scatter.5
  144.1 40.9 reduce-scatter.9
  189.5 228.8 reduce-scatter.7
where the time goes:
time: 425 us
  waiting for transfers between devices  308 us (72%)
  matrix products  68.5 us (16%)
  local copies, waits for them, and re-layouts  18.5 us (4%)
  other arithmetic  16 us (4%)
  between operations  14 us (3%)
    reduce_scatter x1, waiting for transfers between devices, local(): lax.psum_scatter((contract_cols(dquery, w_query) + contract_cols(dkey, w_...  231 us
    dot_general x6, matrix products, contract_cols(): lax.dot_general(left, right, (((1,), (1,)), ((), ())), preferred_element_...  29.4 us
    unnamed x6, waiting for transfers between devices  25.8 us
    dot_general x6, matrix products, contract_rows(): lax.dot_general(left, right, (((0,), (0,)), ((), ())), preferred_element_...  21.5 us
    all_gather x1, waiting for transfers between devices, local(): lax.all_gather(values, 'tm', axis=0, tiled=True)  20.2 us
    reduce_scatter x1, waiting for transfers between devices, local(): lax.psum_scatter(cache_terms.astype(jnp.bfloat16), 'tm', scatter_dimensio...  17.6 us
    unnamed x24, local copies, waits for them, and re-layouts  16.5 us
    all_gather x1, waiting for transfers between devices, local(): lax.all_gather(keys, 'tm', axis=0, tiled=True)  13.5 us
  transfers between devices with their start and end apart: 5, of which 5 were waited for; matrix products, arithmetic and copies ran while one was open for 13% of the time, Pallas kernels for 0%

commit v1 on v0

--- a/solution.py
+++ b/solution.py
@@ -1,7 +1,327 @@
+import functools
+
 import jax
 import jax.numpy as jnp
 from jax import lax
+from jax.experimental import pallas as pl
+from jax.experimental.pallas import tpu as pltpu
 from jax.sharding import PartitionSpec as P
+
+MESH = pl.DeviceIdType.MESH
+BF = jnp.bfloat16
+F32 = jnp.float32
+CHUNKS = (("x", 1024), ("z", 1024), ("x", 1024), ("z", 1024), ("x", 1024))
+NX, NY, NZ = 4, 4, 8
+
+
+def dot_nt(left, right):
+    return lax.dot_general(left, right, (((1,), (1,)), ((), ())), preferred_element_type=F32)
+
+
+def place():
+    t, h = lax.axis_index("tm"), lax.axis_index("head")
+    return lax.div(t, 2), lax.rem(t, 2), lax.div(h, NX), lax.rem(h, NX)
+
+
+def device(y, c, z, x):
+    return (y * 2 + c, z * NX + x)
+
+
+def turn(at, by, n):
+    return lax.rem(at + by + n, n)
+
+
+def peer_on(axis, step):
+    y, c, z, x = place()
+    if axis == "x":
+        return device(y, c, z, turn(x, step, NX))
+    if axis == "y":
+        return device(turn(y, step, NY), c, z, x)
+    if axis == "z":
+        return device(y, c, turn(z, step, NZ), x)
+    return device(y, 1 - c, z, x)
+
+
+class Ring:
+    def __init__(self, axis, n, me, own, land, sems, base):
+        self.axis, self.n, self.me, self.own, self.land = axis, n, me, own, land
+        self.send, self.recv = sems
+        self.ids, count = {}, 0
+        for p in range(n // 2):
+            for way, half in ((0, 0), (1, 1), (0, 1), (1, 0)):
+                if p < self.length(way, half):
+                    self.ids[way, half, p] = count
+                    count += 1
+        self.base = base
+        self.count = count
+
+    def length(self, way, half):
+        return self.n // 2 if way == half else self.n // 2 - 1
+
+    def copy(self, way, half, p):
+        step = (-1, 1)[way]
+        target = turn(self.me, step * (self.length(way, half) - p), self.n)
+        i = self.ids[way, half, p]
+        return target, pltpu.make_async_remote_copy(
+            src_ref=self.own(target, half),
+            dst_ref=self.land.at[i],
+            send_sem=self.send.at[self.base + i],
+            recv_sem=self.recv.at[self.base + i],
+            device_id=peer_on(self.axis, step),
+            device_id_type=MESH,
+        )
+
+    def step(self, p):
+        for way, half in ((0, 0), (1, 1), (0, 1), (1, 0)):
+            if p >= self.length(way, half):
+                continue
+            target, copy = self.copy(way, half, p)
+            if p > 0:
+                self.copy(way, half, p - 1)[1].wait_recv()
+                mine = self.own(target, half)
+                mine[...] = mine[...] + self.land[self.ids[way, half, p - 1]]
+            copy.start()
+
+    def finish(self, write):
+        for half in (0, 1):
+            total = self.own(self.me, half)[...].astype(F32)
+            for way in (0, 1):
+                last = self.length(way, half) - 1
+                self.copy(way, half, last)[1].wait_recv()
+                total = total + self.land[self.ids[way, half, last]].astype(F32)
+            write(half, total)
+
+    def drain(self):
+        for way, half, p in self.ids:
+            self.copy(way, half, p)[1].wait_send()
+
+
+def greet(axes):
+    barrier = pltpu.get_barrier_semaphore()
+    peers = []
+    for axis in axes:
+        peers += [peer_on(axis, 1)] if axis == "c" else [peer_on(axis, -1), peer_on(axis, 1)]
+    for peer in peers:
+        pl.semaphore_signal(barrier, inc=1, device_id=peer, device_id_type=MESH)
+    pl.semaphore_wait(barrier, len(peers))
+
+
+def grads_kernel(
+    tokens_hbm, outg_hbm, wk_hbm, wv_hbm, wq_hbm, d_ref, dt_ref, at_ref,
+    tg_ref, qg_ref, kg_ref, vg_ref, og_ref,
+    tokens, outg, wcat, wp, pair_land, y_land, in_sem, send_sem, recv_sem, *bufs
+):
+    y, c, z, x = place()
+    sems = (send_sem, recv_sem)
+    loads = [
+        pltpu.make_async_copy(src, wcat.at[:, pl.ds(i * 128, 128)], in_sem.at[i])
+        for i, src in enumerate((wk_hbm, wv_hbm, wq_hbm))
+    ]
+    loads += [
+        pltpu.make_async_copy(tokens_hbm, tokens, in_sem.at[3]),
+        pltpu.make_async_copy(outg_hbm, outg, in_sem.at[4]),
+    ]
+    for load in loads:
+        load.start()
+
+    base = 10
+    chunks = []
+    offset = 0
+    for n, (kind, width) in enumerate(CHUNKS):
+        part, land1, mid, land2 = bufs[4 * n : 4 * n + 4]
+        wide = width // 2
+        if kind == "x":
+            first = Ring("x", NX, x, lambda b, h, part=part: part.at[pl.ds(h * 4, 4), b], land1, sems, base)
+            second = Ring(
+                "z", NZ, z, lambda b, h, mid=mid, wide=wide: mid.at[b, :, pl.ds(h * wide, wide)],
+                land2, sems, base + first.count,
+            )
+        else:
+            first = Ring("z", NZ, z, lambda b, h, part=part: part.at[b, pl.ds(h * 2, 2)], land1, sems, base)
+            second = Ring(
+                "x", NX, x, lambda b, h, mid=mid, wide=wide: mid.at[b, :, pl.ds(h * wide, wide)],
+                land2, sems, base + first.count,
+            )
+        base += first.count + second.count
+        chunks.append((kind, width, offset, part, mid, first, second))
+        offset += width
+
+    def token_part(n):
+        kind, width, at, part, mid, first, second = chunks[n]
+
+        def piece(i, _):
+            cols = pl.multiple_of(i * 256, 256)
+            got = dot_nt(d_ref[...], wcat[pl.ds(pl.multiple_of(at + cols, 256), 256), :])
+            part[:, :, :, pl.ds(cols, 256)] = got.astype(BF).reshape(NZ, NX, 16, 256)
+            return 0
+
+        lax.fori_loop(0, width // 256, piece, 0)
+
+    def middle(n):
+        kind, width, at, part, mid, first, second = chunks[n]
+        count = 4 if kind == "x" else 2
+
+        def write(half, total):
+            mid[pl.ds(half * count, count)] = total.astype(BF)
+
+        first.finish(write)
+
+    def end(n):
+        kind, width, at, part, mid, first, second = chunks[n]
+
+        def write(half, total):
+            tg_ref[:, pl.ds(at + half * (width // 2), width // 2)] = total.astype(BF)
+
+        second.finish(write)
+
+    def weight_block(yt, ct):
+        cols = pl.ds(pl.multiple_of((yt * 2 + ct) * 640, 128), 640)
+        top = jnp.dot(dt_ref[...], tokens[:, cols], preferred_element_type=F32)
+        low = jnp.dot(at_ref[...], outg[:, cols], preferred_element_type=F32)
+        return top, low
+
+    def pair_copy(j):
+        yt = turn(y, 2 + 3 * j, NY)
+        return yt, pltpu.make_async_remote_copy(
+            src_ref=wp.at[yt, 1 - c], dst_ref=pair_land.at[yt],
+            send_sem=send_sem.at[j], recv_sem=recv_sem.at[j],
+            device_id=peer_on("c", 1), device_id_type=MESH,
+        )
+
+    def theirs(j, _):
+        yt, copy = pair_copy(j)
+        top, low = weight_block(yt, 1 - c)
+        wp[yt, 1 - c, 0:384, :] = top.astype(BF)
+        wp[yt, 1 - c, 384:512, :] = low.astype(BF)
+        copy.start()
+        return 0
+
+    def ours(j, _):
+        yt, copy = pair_copy(j)
+        top, low = weight_block(yt, c)
+        copy.wait_recv()
+        wp[yt, c, 0:384, :] = (top + pair_land[yt, 0:384, :].astype(F32)).astype(BF)
+        wp[yt, c, 384:512, :] = (low + pair_land[yt, 384:512, :].astype(F32)).astype(BF)
+        return 0
+
+    yring = Ring("y", NY, y, lambda b, h: wp.at[b, c, pl.ds(h * 256, 256)], y_land, sems, 4)
+
+    greet(("x", "z", "y", "c"))
+    for load in loads[:3]:
+        load.wait()
+    firsts = [chunk[5] for chunk in chunks]
+    seconds = [chunk[6] for chunk in chunks]
+    token_part(0)
+    firsts[0].step(0)
+    token_part(1)
+    firsts[1].step(0)
+    loads[3].wait()
+    loads[4].wait()
+    lax.fori_loop(0, 4, theirs, 0)
+    token_part(2)
+    firsts[2].step(0)
+    token_part(3)
+    firsts[3].step(0)
+    lax.fori_loop(0, 4, ours, 0)
+    yring.step(0)
+    firsts[0].step(1)
+    token_part(4)
+    firsts[1].step(1)
+    firsts[4].step(0)
+    firsts[3].step(1)
+    firsts[2].step(1)
+    yring.step(1)
+    firsts[1].step(2)
+    middle(0)
+    seconds[0].step(0)
+    firsts[3].step(2)
+    firsts[4].step(1)
+    seconds[0].step(1)
+    firsts[1].step(3)
+    seconds[0].step(2)
+    firsts[3].step(3)
+    middle(2)
+    seconds[2].step(0)
+    seconds[0].step(3)
+    middle(1)
+    seconds[1].step(0)
+    seconds[2].step(1)
+    middle(3)
+    seconds[3].step(0)
+    middle(4)
+    seconds[4].step(0)
+    seconds[1].step(1)
+    seconds[2].step(2)
+    seconds[4].step(1)
+    seconds[3].step(1)
+    seconds[2].step(3)
+    seconds[4].step(2)
+    end(0)
+    end(1)
+
+    def weights_out(half, total):
+        if half == 0:
+            kg_ref[...] = total[0:128].T.astype(BF)
+            vg_ref[...] = total[128:256].T.astype(BF)
+        else:
+            qg_ref[...] = total[0:128].T.astype(BF)
+            og_ref[...] = total[128:256].astype(BF)
+
+    yring.finish(weights_out)
+    seconds[4].step(3)
+    end(3)
+    end(2)
+    end(4)
+    for j in range(4):
+        pair_copy(j)[1].wait_send()
+    yring.drain()
+    for ring in firsts + seconds:
+        ring.drain()
+
+
+def grads(tokens, out_grad, wk, wv, wq, d, dt, at):
+    bufs = []
+    for kind, width in CHUNKS:
+        bufs.append(pltpu.VMEM((NZ, NX, 16, width), BF))
+        if kind == "x":
+            bufs += [
+                pltpu.VMEM((6, 4, 16, width), BF), pltpu.VMEM((NZ, 16, width), BF),
+                pltpu.VMEM((14, 16, width // 2), BF),
+            ]
+        else:
+            bufs += [
+                pltpu.VMEM((14, 2, 16, width), BF), pltpu.VMEM((NX, 16, width), BF),
+                pltpu.VMEM((6, 16, width // 2), BF),
+            ]
+    count = 10 + 20 * len(CHUNKS)
+    hbm = pl.BlockSpec(memory_space=pl.ANY)
+    vmem = pl.BlockSpec(memory_space=pltpu.VMEM)
+    return pl.pallas_call(
+        grads_kernel,
+        out_shape=(
+            jax.ShapeDtypeStruct((16, 5120), BF),
+            jax.ShapeDtypeStruct((640, 128), BF),
+            jax.ShapeDtypeStruct((640, 128), BF),
+            jax.ShapeDtypeStruct((640, 128), BF),
+            jax.ShapeDtypeStruct((128, 640), BF),
+        ),
+        in_specs=[hbm] * 5 + [vmem] * 3,
+        out_specs=[vmem] * 5,
+        scratch_shapes=[
+            pltpu.VMEM((512, 5120), BF),
+            pltpu.VMEM((512, 5120), BF),
+            pltpu.VMEM((5120, 384), BF),
+            pltpu.VMEM((NY, 2, 512, 640), BF),
+            pltpu.VMEM((NY, 512, 640), BF),
+            pltpu.VMEM((6, 256, 640), BF),
+            pltpu.SemaphoreType.DMA((5,)),
+            pltpu.SemaphoreType.DMA((count,)),
+            pltpu.SemaphoreType.DMA((count,)),
+        ] + bufs,
+        compiler_params=pltpu.CompilerParams(
+            collective_id=1, has_side_effects=True, vmem_limit_bytes=62 * 2**20
+        ),
+    )(tokens, out_grad, wk, wv, wq, d, dt, at)
 
 
 def contract_rows(left, right):
@@ -53,35 +373,8 @@
     ).astype(jnp.float32)
     dkey = summed[:, :width].astype(jnp.bfloat16)
     dvalue = summed[:, width:].astype(jnp.bfloat16)
-    weights_sum = lax.psum_scatter(
-        jnp.concatenate(
-            [
-                contract_rows(tokens, dquery),
-                contract_rows(tokens, dkey),
-                contract_rows(tokens, dvalue),
-                contract_rows(out_grad, attn),
-            ],
-            axis=1,
-        ).astype(jnp.bfloat16),
-        "tm",
-        scatter_dimension=0,
-        tiled=True,
-    ).astype(jnp.float32)
-    query_grad = weights_sum[:, :width].astype(jnp.bfloat16)
-    key_grad = weights_sum[:, width : 2 * width].astype(jnp.bfloat16)
-    value_grad = weights_sum[:, 2 * width : 3 * width].astype(jnp.bfloat16)
-    out_weight_grad = weights_sum[:, 3 * width :].T.astype(jnp.bfloat16)
-    token_grad = lax.psum_scatter(
-        (
-            contract_cols(dquery, w_query)
-            + contract_cols(dkey, w_key)
-            + contract_cols(dvalue, w_value)
-        ).astype(jnp.bfloat16),
-        "head",
-        scatter_dimension=0,
-        tiled=True,
-    )
-    return (token_grad, query_grad, key_grad, value_grad, out_weight_grad)
+    d = jnp.concatenate([dkey, dvalue, dquery], axis=1)
+    return grads(tokens, out_grad, w_key, w_value, w_query, d, d.T, attn.T)
 
 
 def solution(mesh):

time: 425 us -> 203 us (0.48)
  waiting for transfers between devices: 308 us -> 58.8 us
  Pallas kernels: 0 us -> 58.5 us
  matrix products: 68.5 us -> 39.3 us
    reduce_scatter x1 -> x0, waiting for transfers between devices: 231 us -> none  [local(): lax.psum_scatter((contract_cols(dquery, w_query) + contract_cols(dkey, w_...]
    pallas_call x0 -> x1, Pallas kernels: none -> 58.5 us  [grads(): pl.pallas_call(grads_kernel, out_shape=(jax.ShapeDtypeStruct((16, 5120),...]
    unnamed x6 -> x3, waiting for transfers between devices: 25.8 us -> 0.05 us
    dot_general x6 -> x2, matrix products: 21.5 us -> 1.52 us  [contract_rows(): lax.dot_general(left, right, (((0,), (0,)), ((), ())), preferred_element_...]
    dot_general x6 -> x3, matrix products: 29.4 us -> 14.2 us  [contract_cols(): lax.dot_general(left, right, (((1,), (1,)), ((), ())), preferred_element_...]
    reduce_scatter x1, waiting for transfers between devices: 17.6 us -> 25.3 us  [local(): lax.psum_scatter(cache_terms.astype(jnp.bfloat16), 'tm', scatter_dimensio...]
    dot_general x0 -> x1, matrix products: none -> 5.55 us  [local(): jnp.dot(probs_b, value_all, preferred_element_type=jnp.float32)]
    unnamed x24 -> x21, local copies, waits for them, and re-layouts: 16.5 us -> 15.7 us
  transfers between devices with their start and end apart: 5 -> 3, of which waited for: 5 -> 3; matrix products, arithmetic and copies ran while one was open for 13% -> 14% of each run, Pallas kernels for 0% -> 0%
where the time goes in v1:
time: 203 us; the launch traced here: 201 us
  waiting for transfers between devices  58.8 us (29%)
  Pallas kernels  58.5 us (29%)
  matrix products  39.3 us (19%)
  local copies, waits for them, and re-layouts  16.7 us (8%)
  other arithmetic  14.1 us (7%)
  between operations  13.9 us (7%)
    pallas_call x1, Pallas kernels, grads(): pl.pallas_call(grads_kernel, out_shape=(jax.ShapeDtypeStruct((16, 5120),...  58.5 us
    reduce_scatter x1, waiting for transfers between devices, local(): lax.psum_scatter(cache_terms.astype(jnp.bfloat16), 'tm', scatter_dimensio...  25.3 us
    all_gather x1, waiting for transfers between devices, local(): lax.all_gather(values, 'tm', axis=0, tiled=True)  20.2 us
    unnamed x21, local copies, waits for them, and re-layouts  15.7 us
    dot_general x3, matrix products, contract_cols(): lax.dot_general(left, right, (((1,), (1,)), ((), ())), preferred_element_...  14.2 us
    all_gather x1, waiting for transfers between devices, local(): lax.all_gather(keys, 'tm', axis=0, tiled=True)  13.3 us
    convert_element_type x1, other arithmetic, local(): dscore = (probs * (dprobs - delta) * scale).astype(jnp.bfloat16)  8.05 us
    dot_general x1, matrix products, local(): jnp.dot(probs_b, value_all, preferred_element_type=jnp.float32)  5.55 us
  transfers between devices with their start and end apart: 3, of which 3 were waited for; matrix products, arithmetic and copies ran while one was open for 14% of the time, Pallas kernels for 0%

profile of v1, /device:TPU:8, one launch (start us, length us, event | category | flops | bytes accessed | tf_op | source)
XLA Modules:
  0.0 201.3 jit_solution(16399490523753544515)
XLA Ops:
  7.2 0.0 copy-start
  7.2 0.0 copy-start.5
  7.2 0.0 all-gather.3.cloned.1.call-start
  7.2 5.2 %convolution_convert_fusion.5 = bf16[512,128]{1,0:T(8,128)(2,1)} fusion(bf16[512,5120]{1,0:T(8,128)(2,1)} %tokens_hbm.1, bf16[5120,128]{1,0:T(8,128)(2,1)} %wk_hbm.1), kind=kOutput, calls=%fused_computation.16 | convolution fusion | flops 671154176 | bytes 6684672 | tf_op jit(solution)/shard_map/dot_general | solution.py:346
  12.4 0.0 all-gather.3.cloned.1.call-update
  12.5 0.0 all-gather.5.cloned.1.call-start
  12.5 0.0 copy-done.5
  12.5 4.7 %convolution_convert_fusion.3 = bf16[512,128]{1,0:T(8,128)(2,1)} fusion(bf16[512,5120]{1,0:T(8,128)(2,1)} %tokens_hbm.1, bf16[5120,128]{1,0:T(8,128)(2,1)S(1)} %copy-done.5), kind=kOutput, calls=%fused_computation.14 | convolution fusion | flops 671154176 | bytes 6684672 | tf_op jit(solution)/shard_map/dot_general | solution.py:347
  17.2 0.0 all-gather.5.cloned.1.call-update
  17.2 0.0 reduce-scatter.2.cloned.1.call-start
  17.3 0.7 fusion.9
  18.0 0.1 broadcast_bitcast_fusion
  18.0 4.4 %convolution_convert_fusion.6 = bf16[512,128]{1,0:T(8,128)(2,1)S(1)} fusion(bf16[512,5120]{1,0:T(8,128)(2,1)} %tokens_hbm.1, bf16[5120,128]{1,0:T(8,128)(2,1)} %wq_hbm.1), kind=kOutput, calls=%fused_computation.17 | convolution fusion | flops 671154176 | bytes 6684672 | tf_op jit(solution)/shard_map/dot_general | solution.py:345
  22.4 0.0 copy-done
  22.4 4.0 %convolution_convert_fusion.4 = bf16[512,128]{1,0:T(8,128)(2,1)S(1)} fusion(bf16[512,5120]{1,0:T(8,128)(2,1)} %outg_hbm.1, bf16[128,5120]{1,0:T(8,128)(2,1)S(1)} %copy-done), kind=kOutput, calls=%fused_computation.15 | convolution fusion | flops 671154176 | bytes 6684672 | tf_op jit(solution)/shard_map/dot_general | solution.py:334
  26.5 13.3 %all-gather.3.cloned.1.call-done = bf16[4096,128]{1,0:T(8,128)(2,1)} async-done(((bf16[512,128]{1,0:T(8,128)(2,1)}), bf16[4096,128]{1,0:T(8,128)(2,1)}) %all-gather.3.cloned.1.call-update) | async-done | bytes 1048592 | tf_op jit(solution)/shard_map/all_gather | solution.py:351
  39.7 2.7 %fusion = (f32[512]{0:T(512)S(1)}, f32[512,4096]{1,0:T(8,128)S(1)}) fusion(pred[4096]{0:T(1024)(128)(4,1)S(1)} %bitcast.27, bf16[512,128]{1,0:T(8,128)(2,1)S(1)} %convolution_convert_fusion.6, bf16[4096,128]{1,0:T(8,128)(2,1)} %all-gather.3.cloned.1.call-done), kind=kOutput, calls=%fused_computation.4 | convolution fusion | flops 543161856 | bytes 9574400 | tf_op jit(solution)/shard_map/dot_general | solution.py:334
  42.5 0.0 copy-start.3
  42.5 3.2 %copy-done.3 = f32[512,4096]{1,0:T(8,128)} copy-done((f32[512,4096]{1,0:T(8,128)}, f32[512,4096]{1,0:T(8,128)S(1)}, u32[]{:S(2)}) %copy-start.3) | copy-done | bytes 8388632
  45.7 2.2 %fusion.2 = f32[512]{0:T(512)S(1)} fusion(f32[512,4096]{1,0:T(8,128)S(1)} %get-tuple-element.10, f32[512]{0:T(512)S(1)} %get-tuple-element.9, pred[4096]{0:T(1024)(128)(4,1)S(1)} %bitcast.28), kind=kLoop, calls=%fused_computation.6 | loop fusion | flops 8388096 | bytes 8396800 | tf_op jit(solution)/shard_map/reduce_sum | solution.py:361
  47.9 20.2 %all-gather.5.cloned.1.call-done = bf16[4096,128]{1,0:T(8,128)(2,1)} async-done(((bf16[512,128]{1,0:T(8,128)(2,1)}), bf16[4096,128]{1,0:T(8,128)(2,1)}) %all-gather.5.cloned.1.call-update) | async-done | bytes 1048592 | tf_op jit(solution)/shard_map/all_gather | solution.py:352
  68.0 7.4 %multiply_reduce_fusion = (f32[512]{0:T(512)S(1)}, f32[512,4096]{1,0:T(8,128)S(1)}, f32[512,4096]{1,0:T(8,128)}) fusion(f32[512]{0:T(512)S(1)} %fusion.2, f32[512]{0:T(512)S(1)} %get-tuple-element.9, f32[512,4096]{1,0:T(8,128)} %copy-done.3, pred[4096]{0:T(1024)(128)(4,1)S(1)} %bitcast.29, bf16[512,128]{1,0:T(8,128)(2,1)S(1)} %convolution_convert_fusion.4, ...), kind=kOutput, calls=%fused_computation.1 | convolution fusion | flops 549453312 | bytes 26355712 | tf_op jit(solution)/shard_map/dot_general | solution.py:334
  75.5 0.0 copy-start.1
  75.5 0.8 convolution_convert_fusion
  76.2 2.5 %copy-done.1 = f32[512,4096]{1,0:T(8,128)} copy-done((f32[512,4096]{1,0:T(8,128)}, f32[512,4096]{1,0:T(8,128)S(1)}, u32[]{:S(2)}) %copy-start.1) | copy-done | bytes 8388632
  78.7 8.0 %multiply_convert_fusion = bf16[512,4096]{1,0:T(8,128)(2,1)S(1)} fusion(f32[512,4096]{1,0:T(8,128)} %copy-done.1, f32[512,4096]{1,0:T(8,128)} %get-tuple-element.11, f32[512]{0:T(512)S(1)} %get-tuple-element.5), kind=kLoop, calls=%fused_computation | loop fusion | flops 8388608 | bytes 20973568 | tf_op jit(solution)/shard_map/convert_element_type | solution.py:366
  86.7 0.0 copy-start.2
  86.7 1.9 copy-done.2
  88.7 0.8 convolution_convert_fusion.1
  89.5 0.0 copy-start.4
  89.5 1.5 pad_maximum_fusion
  91.0 0.0 copy-start.6
  91.0 0.0 reduce-scatter.2.cloned.1.call-update
  91.0 0.0 copy-done.4
  91.0 3.8 %convolution_convert_fusion.2 = bf16[512,128]{0,1:T(8,128)(2,1)S(1)} fusion(bf16[512,4096]{1,0:T(8,128)(2,1)} %copy-done.2, bf16[4096,128]{1,0:T(8,128)(2,1)S(1)} %copy-done.4), kind=kOutput, calls=%fused_computation.13 | convolution fusion | flops 536936448 | bytes 5373952 | tf_op jit(solution)/shard_map/dot_general | solution.py:367
  94.8 0.0 copy-done.6
  94.8 5.6 %fusion.6.at_ref = bf16[128,512]{1,0:T(8,128)(2,1)} fusion(bf16[4096,128]{1,0:T(8,128)(2,1)S(1)} %copy-done.6, f32[512,4096]{1,0:T(8,128)} %copy-done.1), kind=kOutput, calls=%fused_computation.18 | convolution fusion | flops 539033600 | bytes 9568256 | tf_op jit(solution)/shard_map/dot_general | solution.py:363
  100.3 25.3 %reduce-scatter.2.cloned.1.call-done = bf16[512,256]{0,1:T(8,128)(2,1)} async-done(((bf16[4096,256]{0,1:T(8,128)(2,1)}), bf16[512,256]{0,1:T(8,128)(2,1)}) %reduce-scatter.2.cloned.1.call-update) | async-done | bytes 262160 | tf_op jit(solution)/shard_map/reduce_scatter | solution.py:371
  125.6 1.7 fusion.10
  127.4 0.9 copy.12.d_ref
  128.3 58.5 %shard_map.110 = (bf16[16,5120]{1,0:T(8,128)(2,1)}, bf16[640,128]{1,0:T(8,128)(2,1)}, bf16[640,128]{1,0:T(8,128)(2,1)}, bf16[640,128]{1,0:T(8,128)(2,1)}, bf16[128,640]{1,0:T(8,128)(2,1)}) custom-call(bf16[512,5120]{1,0:T(8,128)(2,1)} %tokens_hbm.1, bf16[512,5120]{1,0:T(8,128)(2,1)} %outg_hbm.1, bf16[5120,128]{1,0:T(8,128)(2,1)} %wk_hbm.1, ...), custom_call_target="tpu_custom_call" | custom-call | tf_op jit(solution)/shard_map/pallas_call | solution.py:299
  186.8 1.6 copy.19
  188.4 1.6 copy.20
  190.0 1.6 copy.21
  191.6 1.6 copy.22
  193.2 1.6 copy.23
  (1 shorter events, 0.0 us)
Async XLA Ops:
  7.2 15.3 %copy-start = (bf16[128,5120]{1,0:T(8,128)(2,1)S(1)}, bf16[128,5120]{1,0:T(8,128)(2,1)}, u32[]{:S(2)}) copy-start(bf16[128,5120]{1,0:T(8,128)(2,1)} %param.11) | copy-start | bytes 3932164
  7.2 5.3 %copy-start.5 = (bf16[5120,128]{1,0:T(8,128)(2,1)S(1)}, bf16[5120,128]{1,0:T(8,128)(2,1)}, u32[]{:S(2)}) copy-start(bf16[5120,128]{1,0:T(8,128)(2,1)} %wv_hbm.1) | copy-start | bytes 3932164
  7.2 32.6 %all-gather.3.cloned.1.call-start = ((), (), s32[]{:S(2)}) async-start(), calls=%async_computation.1 | async-start | bytes 1179648 | tf_op jit(solution)/shard_map/all_gather | solution.py:351
  12.5 55.6 %all-gather.5.cloned.1.call-start = ((), (), s32[]{:S(2)}) async-start(), calls=%async_computation.2 | async-start | bytes 1179648 | tf_op jit(solution)/shard_map/all_gather | solution.py:352
  17.2 108.4 %reduce-scatter.2.cloned.1.call-start = ((), (), s32[]{:S(2)}) async-start(), calls=%async_computation.3 | async-start | bytes 2359296 | tf_op jit(solution)/shard_map/reduce_scatter | solution.py:371
  42.5 3.2 %copy-start.3 = (f32[512,4096]{1,0:T(8,128)}, f32[512,4096]{1,0:T(8,128)S(1)}, u32[]{:S(2)}) copy-start(f32[512,4096]{1,0:T(8,128)S(1)} %get-tuple-element.10) | copy-start | bytes 25165828
  75.5 3.2 %copy-start.1 = (f32[512,4096]{1,0:T(8,128)}, f32[512,4096]{1,0:T(8,128)S(1)}, u32[]{:S(2)}) copy-start(f32[512,4096]{1,0:T(8,128)S(1)} %get-tuple-element.6) | copy-start | bytes 25165828
  86.7 2.0 copy-start.2
  89.5 1.5 copy-start.4
  91.0 3.8 %copy-start.6 = (bf16[4096,128]{1,0:T(8,128)(2,1)S(1)}, bf16[4096,128]{1,0:T(8,128)(2,1)}, u32[]{:S(2)}) copy-start(bf16[4096,128]{1,0:T(8,128)(2,1)} %all-gather.5.cloned.1.call-done) | copy-start | bytes 3145732
Sparse Core Ops, SparseCore 0:
  12.6 27.1 all-gather.2
  42.2 25.7 all-gather.4
  91.1 34.4 reduce-scatter.1

commit v2 on v1

--- a/solution.py
+++ b/solution.py
@@ -1,5 +1,3 @@
-import functools
-
 import jax
 import jax.numpy as jnp
 from jax import lax
@@ -12,10 +10,15 @@
 F32 = jnp.float32
 CHUNKS = (("x", 1024), ("z", 1024), ("x", 1024), ("z", 1024), ("x", 1024))
 NX, NY, NZ = 4, 4, 8
+GATHER = 10 + 20 * len(CHUNKS)
 
 
 def dot_nt(left, right):
     return lax.dot_general(left, right, (((1,), (1,)), ((), ())), preferred_element_type=F32)
+
+
+def dot_tn(left, right):
+    return lax.dot_general(left, right, (((0,), (0,)), ((), ())), preferred_element_type=F32)
 
 
 def place():
@@ -107,22 +110,187 @@
 
 
 def grads_kernel(
-    tokens_hbm, outg_hbm, wk_hbm, wv_hbm, wq_hbm, d_ref, dt_ref, at_ref,
+    tokens_hbm, outg_hbm, wk_hbm, wv_hbm, wq_hbm, wo_hbm, lists_ref,
     tg_ref, qg_ref, kg_ref, vg_ref, og_ref,
-    tokens, outg, wcat, wp, pair_land, y_land, in_sem, send_sem, recv_sem, *bufs
+    tokens, outg, wcat, wout, kv, query, d_attn, scores, dprobs, top_ref, sum_ref, del_ref, atf, dqf,
+    cache, cache_pair, cache_land, d_ref, dt_ref, at_ref,
+    wp, pair_land, y_land, in_sem, send_sem, recv_sem, *bufs
 ):
     y, c, z, x = place()
     sems = (send_sem, recv_sem)
+    me = y * 2 + c
+    scale = 1.0 / 128**0.5
     loads = [
-        pltpu.make_async_copy(src, wcat.at[:, pl.ds(i * 128, 128)], in_sem.at[i])
-        for i, src in enumerate((wk_hbm, wv_hbm, wq_hbm))
-    ]
-    loads += [
-        pltpu.make_async_copy(tokens_hbm, tokens, in_sem.at[3]),
-        pltpu.make_async_copy(outg_hbm, outg, in_sem.at[4]),
+        pltpu.make_async_copy(src, dst, in_sem.at[i])
+        for i, (src, dst) in enumerate((
+            (wk_hbm, wcat.at[:, pl.ds(0, 128)]), (wv_hbm, wcat.at[:, pl.ds(128, 128)]), (tokens_hbm, tokens),
+            (wq_hbm, wcat.at[:, pl.ds(256, 128)]), (outg_hbm, outg), (wo_hbm, wout),
+        ))
     ]
     for load in loads:
         load.start()
+
+    def block(dy, core):
+        return turn(y, dy, NY) * 2 + core
+
+    def move(i, blk, rows, axis, step):
+        ref = kv.at[blk, rows]
+        return pltpu.make_async_remote_copy(
+            src_ref=ref, dst_ref=ref,
+            send_sem=send_sem.at[GATHER + i], recv_sem=recv_sem.at[GATHER + i],
+            device_id=peer_on(axis, step), device_id_type=MESH,
+        )
+
+    low, high, whole = pl.ds(0, 256), pl.ds(256, 256), pl.ds(0, 512)
+    near = [
+        move(0, me, low, "y", 1), move(3, me, high, "y", -1),
+        move(1, me, high, "y", 1), move(2, me, low, "y", -1),
+    ]
+    far = [move(4, block(3, c), low, "y", 1), move(5, block(1, c), high, "y", -1)]
+    across = [move(6 + dy, block(dy, c), whole, "c", 1) for dy in range(4)]
+
+    def span(k):
+        return pl.ds(pl.multiple_of(k * 640, 128), 640)
+
+    def project_kv(k, _):
+        scores[0, :, 0:256] += jnp.dot(tokens[:, span(k)], wcat[span(k), 0:256], preferred_element_type=F32)
+        return 0
+
+    def project_rest(k, _):
+        scores[0, :, 0:128] += jnp.dot(tokens[:, span(k)], wcat[span(k), 256:384], preferred_element_type=F32)
+        scores[0, :, 128:256] += dot_nt(outg[:, span(k)], wout[:, span(k)])
+        return 0
+
+    greet(("x", "z", "y", "c"))
+    scores[0] = jnp.zeros((512, 512), F32)
+    for load in loads[:3]:
+        load.wait()
+    lax.fori_loop(0, 8, project_kv, 0)
+    kv[me] = scores[0, :, 0:256].astype(BF)
+    for copy in near:
+        copy.start()
+    across[0].start()
+    scores[0] = jnp.zeros((512, 512), F32)
+    for load in loads[3:]:
+        load.wait()
+    lax.fori_loop(0, 8, project_rest, 0)
+    query[...] = scores[0, :, 0:128].astype(BF)
+    d_attn[...] = scores[0, :, 128:256].astype(BF)
+    top_ref[...] = jnp.full((1, 512), -3e30, F32)
+    sum_ref[...] = jnp.zeros((1, 512), F32)
+    del_ref[...] = jnp.zeros((1, 512), F32)
+    atf[...] = jnp.zeros((128, 512), F32)
+    dqf[...] = jnp.zeros((128, 512), F32)
+
+    def score(i, _):
+        pair, other = lax.div(i, 2), lax.rem(i, 2)
+        dy = jnp.where(pair == 1, 3, jnp.where(pair == 2, 1, jnp.where(pair == 3, 2, 0)))
+        b = block(dy, jnp.where(other == 1, 1 - c, c))
+
+        @pl.when(i == 1)
+        def _():
+            across[0].wait_recv()
+
+        @pl.when(i == 2)
+        def _():
+            near[0].wait_recv()
+            far[0].start()
+            near[1].wait_recv()
+            far[1].start()
+            near[2].wait_recv()
+            across[3].start()
+            near[3].wait_recv()
+            across[1].start()
+
+        @pl.when(i == 3)
+        def _():
+            across[3].wait_recv()
+
+        @pl.when(i == 5)
+        def _():
+            across[1].wait_recv()
+
+        @pl.when(i == 6)
+        def _():
+            far[0].wait_recv()
+            far[1].wait_recv()
+            across[2].start()
+
+        @pl.when(i == 7)
+        def _():
+            across[2].wait_recv()
+
+        seen = (b == me) | ((b < me) & (lists_ref[me, b] == 1))
+        shut = jnp.where(seen, 0.0, -1e30).astype(F32)
+        got = dot_nt(kv[b, :, 0:128], query[...]) * scale + shut
+        scores[b] = got
+        top_ref[...] = jnp.maximum(top_ref[...], jnp.max(got, axis=0, keepdims=True))
+        dprobs[b] = dot_nt(kv[b, :, 128:256], d_attn[...])
+        return 0
+
+    lax.fori_loop(0, 8, score, 0)
+
+    def weigh(b, _):
+        got = jnp.exp(scores[b] - top_ref[...])
+        scores[b] = got
+        sum_ref[...] += jnp.sum(got, axis=0, keepdims=True)
+        del_ref[...] += jnp.sum(got * dprobs[b], axis=0, keepdims=True)
+        return 0
+
+    lax.fori_loop(0, 8, weigh, 0)
+    sum_ref[...] = 1.0 / sum_ref[...]
+    del_ref[...] = del_ref[...] * sum_ref[...]
+
+    def cache_block(b):
+        probs = scores[b] * sum_ref[...]
+        probs_b = probs.astype(BF)
+        dscore = (probs * (dprobs[b] - del_ref[...]) * scale).astype(BF)
+        atf[...] += dot_tn(kv[b, :, 128:256], probs_b)
+        dqf[...] += dot_tn(kv[b, :, 0:128], dscore)
+        dk = jnp.dot(dscore, query[...], preferred_element_type=F32)
+        dv = jnp.dot(probs_b, d_attn[...], preferred_element_type=F32)
+        return dk, dv
+
+    def cache_copy(j):
+        yt = turn(y, 2 + 3 * j, NY)
+        return yt, pltpu.make_async_remote_copy(
+            src_ref=cache.at[yt, 1 - c], dst_ref=cache_pair.at[yt],
+            send_sem=send_sem.at[GATHER + 10 + j], recv_sem=recv_sem.at[GATHER + 10 + j],
+            device_id=peer_on("c", 1), device_id_type=MESH,
+        )
+
+    def cache_theirs(j, _):
+        yt, copy = cache_copy(j)
+        dk, dv = cache_block(yt * 2 + 1 - c)
+        cache[yt, 1 - c, :, 0:128] = dk.astype(BF)
+        cache[yt, 1 - c, :, 128:256] = dv.astype(BF)
+        copy.start()
+        return 0
+
+    def cache_ours(j, _):
+        yt, copy = cache_copy(j)
+        dk, dv = cache_block(yt * 2 + c)
+        copy.wait_recv()
+        cache[yt, c, :, 0:128] = (dk + cache_pair[yt, :, 0:128].astype(F32)).astype(BF)
+        cache[yt, c, :, 128:256] = (dv + cache_pair[yt, :, 128:256].astype(F32)).astype(BF)
+        return 0
+
+    lax.fori_loop(0, 4, cache_theirs, 0)
+    lax.fori_loop(0, 4, cache_ours, 0)
+    cring = Ring(
+        "y", NY, y, lambda b, h: cache.at[b, c, pl.ds(h * 256, 256)], cache_land, sems, GATHER + 14
+    )
+    cring.step(0)
+    at_ref[...] = atf[...].astype(BF)
+    dt_ref[256:384, :] = dqf[...].astype(BF)
+    d_ref[:, 256:384] = dqf[...].T.astype(BF)
+    cring.step(1)
+
+    def cache_out(half, total):
+        d_ref[half * 256 : half * 256 + 256, 0:256] = total.astype(BF)
+        dt_ref[0:256, half * 256 : half * 256 + 256] = total.T.astype(BF)
+
+    cring.finish(cache_out)
 
     base = 10
     chunks = []
@@ -206,17 +374,12 @@
 
     yring = Ring("y", NY, y, lambda b, h: wp.at[b, c, pl.ds(h * 256, 256)], y_land, sems, 4)
 
-    greet(("x", "z", "y", "c"))
-    for load in loads[:3]:
-        load.wait()
     firsts = [chunk[5] for chunk in chunks]
     seconds = [chunk[6] for chunk in chunks]
     token_part(0)
     firsts[0].step(0)
     token_part(1)
     firsts[1].step(0)
-    loads[3].wait()
-    loads[4].wait()
     lax.fori_loop(0, 4, theirs, 0)
     token_part(2)
     firsts[2].step(0)
@@ -274,12 +437,17 @@
     end(4)
     for j in range(4):
         pair_copy(j)[1].wait_send()
+    for copy in near + far + across:
+        copy.wait_send()
+    for j in range(4):
+        cache_copy(j)[1].wait_send()
+    cring.drain()
     yring.drain()
     for ring in firsts + seconds:
         ring.drain()
 
 
-def grads(tokens, out_grad, wk, wv, wq, d, dt, at):
+def local(tokens, w_query, w_key, w_value, w_out, out_grad, frame_lists):
     bufs = []
     for kind, width in CHUNKS:
         bufs.append(pltpu.VMEM((NZ, NX, 16, width), BF))
@@ -293,7 +461,7 @@
                 pltpu.VMEM((14, 2, 16, width), BF), pltpu.VMEM((NX, 16, width), BF),
                 pltpu.VMEM((6, 16, width // 2), BF),
             ]
-    count = 10 + 20 * len(CHUNKS)
+    count = GATHER + 20
     hbm = pl.BlockSpec(memory_space=pl.ANY)
     vmem = pl.BlockSpec(memory_space=pltpu.VMEM)
     return pl.pallas_call(
@@ -305,76 +473,40 @@
             jax.ShapeDtypeStruct((640, 128), BF),
             jax.ShapeDtypeStruct((128, 640), BF),
         ),
-        in_specs=[hbm] * 5 + [vmem] * 3,
+        in_specs=[hbm] * 6 + [pl.BlockSpec(memory_space=pltpu.SMEM)],
         out_specs=[vmem] * 5,
         scratch_shapes=[
             pltpu.VMEM((512, 5120), BF),
             pltpu.VMEM((512, 5120), BF),
             pltpu.VMEM((5120, 384), BF),
+            pltpu.VMEM((128, 5120), BF),
+            pltpu.VMEM((8, 512, 256), BF),
+            pltpu.VMEM((512, 128), BF),
+            pltpu.VMEM((512, 128), BF),
+            pltpu.VMEM((8, 512, 512), F32),
+            pltpu.VMEM((8, 512, 512), F32),
+            pltpu.VMEM((1, 512), F32),
+            pltpu.VMEM((1, 512), F32),
+            pltpu.VMEM((1, 512), F32),
+            pltpu.VMEM((128, 512), F32),
+            pltpu.VMEM((128, 512), F32),
+            pltpu.VMEM((NY, 2, 512, 256), BF),
+            pltpu.VMEM((NY, 512, 256), BF),
+            pltpu.VMEM((6, 256, 256), BF),
+            pltpu.VMEM((512, 384), BF),
+            pltpu.VMEM((384, 512), BF),
+            pltpu.VMEM((128, 512), BF),
             pltpu.VMEM((NY, 2, 512, 640), BF),
             pltpu.VMEM((NY, 512, 640), BF),
             pltpu.VMEM((6, 256, 640), BF),
-            pltpu.SemaphoreType.DMA((5,)),
+            pltpu.SemaphoreType.DMA((6,)),
             pltpu.SemaphoreType.DMA((count,)),
             pltpu.SemaphoreType.DMA((count,)),
         ] + bufs,
         compiler_params=pltpu.CompilerParams(
-            collective_id=1, has_side_effects=True, vmem_limit_bytes=62 * 2**20
+            collective_id=1, has_side_effects=True, vmem_limit_bytes=67_000_000
         ),
-    )(tokens, out_grad, wk, wv, wq, d, dt, at)
-
-
-def contract_rows(left, right):
-    return lax.dot_general(
-        left, right, (((0,), (0,)), ((), ())), preferred_element_type=jnp.float32
-    )
-
-
-def contract_cols(left, right):
-    return lax.dot_general(
-        left, right, (((1,), (1,)), ((), ())), preferred_element_type=jnp.float32
-    )
-
-
-def local(tokens, w_query, w_key, w_value, w_out, out_grad, frame_lists):
-    width = w_query.shape[1]
-    scale = 1.0 / width**0.5
-    rows = tokens.shape[0]
-    groups = lax.axis_size("tm")
-    mine = lax.axis_index("tm")
-    query = jnp.dot(tokens, w_query, preferred_element_type=jnp.float32).astype(jnp.bfloat16)
-    keys = jnp.dot(tokens, w_key, preferred_element_type=jnp.float32).astype(jnp.bfloat16)
-    values = jnp.dot(tokens, w_value, preferred_element_type=jnp.float32).astype(jnp.bfloat16)
-    d_attn = contract_cols(out_grad, w_out).astype(jnp.bfloat16)
-    my_list = lax.dynamic_slice_in_dim(frame_lists, mine, 1, 0)[0]
-    key_all, value_all = (
-        lax.all_gather(keys, "tm", axis=0, tiled=True),
-        lax.all_gather(values, "tm", axis=0, tiled=True),
-    )
-    order = jnp.arange(groups, dtype=jnp.int32)
-    allowed = (order == mine) | (my_list == 1) & (order < mine)
-    key_mask = jnp.repeat(allowed, rows)[None, :]
-    scores = contract_cols(query, key_all) * scale
-    scores = jnp.where(key_mask, scores, jnp.float32(-1e30))
-    top = jnp.max(scores, axis=1, keepdims=True)
-    expd = jnp.exp(scores - top)
-    probs = expd / jnp.sum(expd, axis=1, keepdims=True)
-    probs_b = probs.astype(jnp.bfloat16)
-    attn = jnp.dot(probs_b, value_all, preferred_element_type=jnp.float32).astype(jnp.bfloat16)
-    dprobs = contract_cols(d_attn, value_all)
-    delta = jnp.sum(probs * dprobs, axis=1, keepdims=True)
-    dscore = (probs * (dprobs - delta) * scale).astype(jnp.bfloat16)
-    dquery = jnp.dot(dscore, key_all, preferred_element_type=jnp.float32).astype(jnp.bfloat16)
-    cache_terms = jnp.concatenate(
-        [contract_rows(dscore, query), contract_rows(probs_b, d_attn)], axis=1
-    )
-    summed = lax.psum_scatter(
-        cache_terms.astype(jnp.bfloat16), "tm", scatter_dimension=0, tiled=True
-    ).astype(jnp.float32)
-    dkey = summed[:, :width].astype(jnp.bfloat16)
-    dvalue = summed[:, width:].astype(jnp.bfloat16)
-    d = jnp.concatenate([dkey, dvalue, dquery], axis=1)
-    return grads(tokens, out_grad, w_key, w_value, w_query, d, d.T, attn.T)
+    )(tokens, out_grad, w_key, w_value, w_query, w_out, frame_lists)
 
 
 def solution(mesh):

time: 203 us -> 103 us (0.51)
  waiting for transfers between devices: 58.8 us -> 0 us
  matrix products: 39.3 us -> 0 us
  Pallas kernels: 58.5 us -> 93.6 us
  other arithmetic: 14.1 us -> 0 us
  between operations: 13.9 us -> 0.65 us
  local copies, waits for them, and re-layouts: 16.7 us -> 7.08 us
    dot_general x10 -> x0, matrix products: 39.3 us -> none  [the longest x3 14.2 us: contract_cols(): lax.dot_general(left, right, (((1,), (1,)), ((), ())), preferred_element_...]
    pallas_call x1, Pallas kernels: 58.5 us -> 93.6 us  [local(): pl.pallas_call(grads_kernel, out_shape=(jax.ShapeDtypeStruct((16, 5120),...]
    all_gather x2 -> x0, waiting for transfers between devices: 33.4 us -> none  [the longest x1 20.2 us: local(): lax.all_gather(values, 'tm', axis=0, tiled=True)]
    reduce_scatter x1 -> x0, waiting for transfers between devices: 25.3 us -> none  [local(): lax.psum_scatter(cache_terms.astype(jnp.bfloat16), 'tm', scatter_dimensio...]
    unnamed x21 -> x7, local copies, waits for them, and re-layouts: 15.7 us -> 7.08 us
    convert_element_type x1 -> x0, other arithmetic: 8.05 us -> none  [local(): dscore = (probs * (dprobs - delta) * scale).astype(jnp.bfloat16)]
    reduce_sum x1 -> x0, other arithmetic: 2.15 us -> none  [local(): probs = expd / jnp.sum(expd, axis=1, keepdims=True)]
  transfers between devices with their start and end apart: 3 -> 0, of which waited for: 3 -> 0; matrix products, arithmetic and copies ran while one was open for 14% -> 0% of each run, Pallas kernels for 0% -> 0%
where the time goes in v2:
time: 103 us; the launch traced here: 101 us
  Pallas kernels  93.6 us (91%)
  local copies, waits for them, and re-layouts  7.08 us (7%)
    pallas_call x1, Pallas kernels, local(): pl.pallas_call(grads_kernel, out_shape=(jax.ShapeDtypeStruct((16, 5120),...  93.6 us
    unnamed x7, local copies, waits for them, and re-layouts  7.08 us

profile of v2, /device:TPU:8, one launch (start us, length us, event | category | flops | bytes accessed | tf_op | source)
XLA Modules:
  0.0 101.3 jit_solution(588904271810528994)
XLA Ops:
  0.6 93.6 %shard_map.110 = (bf16[16,5120]{1,0:T(8,128)(2,1)}, bf16[640,128]{1,0:T(8,128)(2,1)}, bf16[640,128]{1,0:T(8,128)(2,1)}, bf16[640,128]{1,0:T(8,128)(2,1)}, bf16[128,640]{1,0:T(8,128)(2,1)}) custom-call(bf16[512,5120]{1,0:T(8,128)(2,1)} %tokens_hbm.1, bf16[512,5120]{1,0:T(8,128)(2,1)} %outg_hbm.1, bf16[5120,128]{1,0:T(8,128)(2,1)} %wk_hbm.1, ...), custom_call_target="tpu_custom_call" | custom-call | tf_op jit(solution)/shard_map/pallas_call | solution.py:467
  94.2 0.0 copy-start
  94.2 1.6 %copy.17 = bf16[16,5120]{1,0:T(8,128)(2,1)} copy(bf16[16,5120]{1,0:T(8,128)(2,1)} %get-tuple-element.10) | data formatting | bytes 327680
  95.9 1.6 %copy.18 = bf16[640,128]{1,0:T(8,128)(2,1)} copy(bf16[640,128]{1,0:T(8,128)(2,1)} %get-tuple-element.11) | data formatting | bytes 327680
  97.5 1.6 %copy.19 = bf16[640,128]{1,0:T(8,128)(2,1)} copy(bf16[640,128]{1,0:T(8,128)(2,1)} %get-tuple-element.12) | data formatting | bytes 327680
  99.0 1.6 %copy.20 = bf16[640,128]{1,0:T(8,128)(2,1)} copy(bf16[640,128]{1,0:T(8,128)(2,1)} %get-tuple-element.13) | data formatting | bytes 327680
  100.6 0.0 copy-done
  100.6 0.7 copy.21
Async XLA Ops:
  94.2 6.4 %copy-start = (bf16[128,640]{1,0:T(8,128)(2,1)S(1)}, bf16[128,640]{1,0:T(8,128)(2,1)}, u32[]{:S(2)}) copy-start(bf16[128,640]{1,0:T(8,128)(2,1)} %get-tuple-element.14) | copy-start | bytes 491524

commit v3 on v2

--- a/solution.py
+++ b/solution.py
@@ -10,6 +10,8 @@
 F32 = jnp.float32
 CHUNKS = (("x", 1024), ("z", 1024), ("x", 1024), ("z", 1024), ("x", 1024))
 NX, NY, NZ = 4, 4, 8
+ORDER = sum(j << 2 * i for i, j in enumerate((0, 1, 0, 3, 1, 3, 2, 2)))
+OURS = sum(1 << i for i in (2, 4, 5, 7))
 GATHER = 10 + 20 * len(CHUNKS)
 
 
@@ -259,32 +261,60 @@
             device_id=peer_on("c", 1), device_id_type=MESH,
         )
 
-    def cache_theirs(j, _):
-        yt, copy = cache_copy(j)
-        dk, dv = cache_block(yt * 2 + 1 - c)
-        cache[yt, 1 - c, :, 0:128] = dk.astype(BF)
-        cache[yt, 1 - c, :, 128:256] = dv.astype(BF)
-        copy.start()
-        return 0
-
-    def cache_ours(j, _):
-        yt, copy = cache_copy(j)
-        dk, dv = cache_block(yt * 2 + c)
-        copy.wait_recv()
-        cache[yt, c, :, 0:128] = (dk + cache_pair[yt, :, 0:128].astype(F32)).astype(BF)
-        cache[yt, c, :, 128:256] = (dv + cache_pair[yt, :, 128:256].astype(F32)).astype(BF)
-        return 0
-
-    lax.fori_loop(0, 4, cache_theirs, 0)
-    lax.fori_loop(0, 4, cache_ours, 0)
     cring = Ring(
         "y", NY, y, lambda b, h: cache.at[b, c, pl.ds(h * 256, 256)], cache_land, sems, GATHER + 14
     )
-    cring.step(0)
+
+    def cache_step(i, _):
+        j = lax.shift_right_logical(jnp.int32(ORDER), 2 * i) & 3
+        ours = (lax.shift_right_logical(jnp.int32(OURS), i) & 1) == 1
+        yt, copy = cache_copy(j)
+        dk, dv = cache_block(yt * 2 + jnp.where(ours, c, 1 - c))
+
+        @pl.when(jnp.logical_not(ours))
+        def _():
+            cache[yt, 1 - c, :, 0:128] = dk.astype(BF)
+            cache[yt, 1 - c, :, 128:256] = dv.astype(BF)
+            copy.start()
+
+        @pl.when(ours)
+        def _():
+            copy.wait_recv()
+            cache[yt, c, :, 0:128] = (dk + cache_pair[yt, :, 0:128].astype(F32)).astype(BF)
+            cache[yt, c, :, 128:256] = (dv + cache_pair[yt, :, 128:256].astype(F32)).astype(BF)
+
+        @pl.when(i == 2)
+        def _():
+            cring.copy(0, 0, 0)[1].start()
+            cring.copy(1, 1, 0)[1].start()
+
+        @pl.when(i == 4)
+        def _():
+            cring.copy(1, 0, 0)[1].start()
+
+        @pl.when(i == 5)
+        def _():
+            cring.copy(0, 1, 0)[1].start()
+
+        @pl.when(i == 6)
+        def _():
+            cring.step(1)
+
+        return 0
+
+    lax.fori_loop(0, 8, cache_step, 0)
     at_ref[...] = atf[...].astype(BF)
     dt_ref[256:384, :] = dqf[...].astype(BF)
     d_ref[:, 256:384] = dqf[...].T.astype(BF)
-    cring.step(1)
+
+    def early(i, _):
+        cols = pl.ds(pl.multiple_of(i * 640, 128), 640)
+        yt, ct = lax.div(i, 2), lax.rem(i, 2)
+        wp[yt, ct, 256:384, :] = jnp.dot(dt_ref[256:384, :], tokens[:, cols], preferred_element_type=F32).astype(BF)
+        wp[yt, ct, 384:512, :] = jnp.dot(at_ref[...], outg[:, cols], preferred_element_type=F32).astype(BF)
+        return 0
+
+    lax.fori_loop(0, 8, early, 0)
 
     def cache_out(half, total):
         d_ref[half * 256 : half * 256 + 256, 0:256] = total.astype(BF)
@@ -344,9 +374,7 @@
 
     def weight_block(yt, ct):
         cols = pl.ds(pl.multiple_of((yt * 2 + ct) * 640, 128), 640)
-        top = jnp.dot(dt_ref[...], tokens[:, cols], preferred_element_type=F32)
-        low = jnp.dot(at_ref[...], outg[:, cols], preferred_element_type=F32)
-        return top, low
+        return jnp.dot(dt_ref[0:256, :], tokens[:, cols], preferred_element_type=F32)
 
     def pair_copy(j):
         yt = turn(y, 2 + 3 * j, NY)
@@ -358,18 +386,16 @@
 
     def theirs(j, _):
         yt, copy = pair_copy(j)
-        top, low = weight_block(yt, 1 - c)
-        wp[yt, 1 - c, 0:384, :] = top.astype(BF)
-        wp[yt, 1 - c, 384:512, :] = low.astype(BF)
+        wp[yt, 1 - c, 0:256, :] = weight_block(yt, 1 - c).astype(BF)
         copy.start()
         return 0
 
     def ours(j, _):
         yt, copy = pair_copy(j)
-        top, low = weight_block(yt, c)
+        top = weight_block(yt, c)
         copy.wait_recv()
-        wp[yt, c, 0:384, :] = (top + pair_land[yt, 0:384, :].astype(F32)).astype(BF)
-        wp[yt, c, 384:512, :] = (low + pair_land[yt, 384:512, :].astype(F32)).astype(BF)
+        wp[yt, c, 0:256, :] = (top + pair_land[yt, 0:256, :].astype(F32)).astype(BF)
+        wp[yt, c, 256:512, :] = wp[yt, c, 256:512, :] + pair_land[yt, 256:512, :]
         return 0
 
     yring = Ring("y", NY, y, lambda b, h: wp.at[b, c, pl.ds(h * 256, 256)], y_land, sems, 4)

time: 103 us -> 97.9 us (0.950)
  Pallas kernels: 93.6 us -> 88.3 us
    pallas_call x1, Pallas kernels: 93.6 us -> 88.3 us  [local(): pl.pallas_call(grads_kernel, out_shape=(jax.ShapeDtypeStruct((16, 5120),...]
where the time goes in v3:
time: 97.9 us; the launch traced here: 96 us
  Pallas kernels  88.3 us (90%)
  local copies, waits for them, and re-layouts  7.08 us (7%)
    pallas_call x1, Pallas kernels, local(): pl.pallas_call(grads_kernel, out_shape=(jax.ShapeDtypeStruct((16, 5120),...  88.3 us
    unnamed x7, local copies, waits for them, and re-layouts  7.08 us

profile of v3, /device:TPU:8, one launch (start us, length us, event | category | flops | bytes accessed | tf_op | source)
XLA Modules:
  0.0 96.0 jit_solution(17968630369122429576)
XLA Ops:
  0.6 88.3 %shard_map.110 = (bf16[16,5120]{1,0:T(8,128)(2,1)}, bf16[640,128]{1,0:T(8,128)(2,1)}, bf16[640,128]{1,0:T(8,128)(2,1)}, bf16[640,128]{1,0:T(8,128)(2,1)}, bf16[128,640]{1,0:T(8,128)(2,1)}) custom-call(bf16[512,5120]{1,0:T(8,128)(2,1)} %tokens_hbm.1, bf16[512,5120]{1,0:T(8,128)(2,1)} %outg_hbm.1, bf16[5120,128]{1,0:T(8,128)(2,1)} %wk_hbm.1, ...), custom_call_target="tpu_custom_call" | custom-call | tf_op jit(solution)/shard_map/pallas_call | solution.py:493
  88.9 0.0 copy-start
  88.9 1.6 %copy.17 = bf16[16,5120]{1,0:T(8,128)(2,1)} copy(bf16[16,5120]{1,0:T(8,128)(2,1)} %get-tuple-element.10) | data formatting | bytes 327680
  90.6 1.6 %copy.18 = bf16[640,128]{1,0:T(8,128)(2,1)} copy(bf16[640,128]{1,0:T(8,128)(2,1)} %get-tuple-element.11) | data formatting | bytes 327680
  92.1 1.6 %copy.19 = bf16[640,128]{1,0:T(8,128)(2,1)} copy(bf16[640,128]{1,0:T(8,128)(2,1)} %get-tuple-element.12) | data formatting | bytes 327680
  93.7 1.6 %copy.20 = bf16[640,128]{1,0:T(8,128)(2,1)} copy(bf16[640,128]{1,0:T(8,128)(2,1)} %get-tuple-element.13) | data formatting | bytes 327680
  95.3 0.0 copy-done
  95.3 0.7 copy.21
Async XLA Ops:
  88.9 6.4 %copy-start = (bf16[128,640]{1,0:T(8,128)(2,1)S(1)}, bf16[128,640]{1,0:T(8,128)(2,1)}, u32[]{:S(2)}) copy-start(bf16[128,640]{1,0:T(8,128)(2,1)} %get-tuple-element.14) | copy-start | bytes 491524
